TPU v7x, 32 devices: a whole 2x2x4 slice. The times are simulated.
32 devices in a mesh: groups: 2 (over y), rows: 4 (over z), cols: 2 (over x), sub: 2 (over core).
Axes of the slice: x: 2, y: 2, z: 4, core: 2. Of those that a mesh axis runs over, the one named last changes fastest.
Arguments:
- elevation: float32 [256, 16384], P(('groups', 'rows', 'sub'), 'cols'), parts along dimension 0, may hold values from -6 to 6
- fill_depth: float32 [256, 16384], P(('groups', 'rows', 'sub'), 'cols'), parts along dimension 0, may hold values from 0.5 to 4
- edge_rows: int32 [4, 16384], P('groups', 'cols'), parts along dimension 0, may hold values 0 or 1
- edge_sides: int32 [4, 128], P('groups', ('rows', 'sub')), parts along dimension 0, may hold values 0 or 1
- adjacency: int32 [16, 6], P('groups'), parts along dimension 0, may hold values from 0 to 7
Outputs:
- filled: float32 [256, 16384], P(('groups', 'rows', 'sub'), 'cols'), parts along dimension 0
There are 2 independent parts, one for each index of `groups`. A program takes and returns all parts, laid end to end along the dimension named above; each array names one. Nothing has to cross between parts.
Inputs may be any that keep to these rules, and one draw needn't show every extreme that they name: `adjacency`: tile numbers count tiles row by row.
All inputs are finite; a program needn't handle non-finite values. No bound on the sum of `edge_rows` or of `edge_sides` on one device may be relied on, other than what follows from the above.
Results may differ from a plain program's by a relative error of at most 0.00002.
Values sent between devices are 32-bit elements; how exact they have to be, the bound alone decides.
A program may use at most 64 MiB of HBM per device.

v0:
```python
import functools

import jax
import jax.numpy as jnp
from jax import lax
from jax.experimental import pallas as pl
from jax.experimental.pallas import tpu as pltpu
from jax.sharding import PartitionSpec as P

PASSES = 8
ROUNDS = 4

unreached = 1000000000.0
rise_step = 0.01
hop_rise = 0.05
spill_lift = 3.0

DEPTH = 4
SUBL = 8
TILE = 128
HALF = TILE // 2
MESH = pl.DeviceIdType.MESH


def kernel(
    sizes, elev_hbm, fill_hbm, edge_hbm, side_hbm, adj_hbm, out_hbm,
    ground, fill, first, second, third, ping, pong, done,
    edge, side, adj, ring_own, ring_low, ring_high,
    mine, gathered, hops, levels, even, odd, seam_ground,
    load_sem, send_sem, recv_sem, level_send, level_recv, out_sem,
):
    n_groups, n_rows, n_cols, n_sub = sizes
    height, width = elev_hbm.shape
    chunk = width // SUBL
    lanes = chunk + TILE
    low, high = DEPTH, DEPTH + height
    total = height + 2 * DEPTH
    n_tiles = adj.shape[0]
    padded = mine.shape[1]
    members = n_rows * n_cols * n_sub

    group = lax.axis_index("groups")
    tile_row = lax.axis_index("rows")
    col = lax.axis_index("cols")
    sub = lax.axis_index("sub")
    band = tile_row * n_sub + sub
    bands = n_rows * n_sub
    me = (tile_row * n_cols + col) * n_sub + sub

    near = 1 - 2 * (band % 2)
    far = -near

    def has(dr):
        return jnp.logical_and(band + dr >= 0, band + dr < bands)

    has_col = {-1: col > 0, 1: col < n_cols - 1}

    def both(dr, dc):
        if dc == 0:
            return has(dr)
        if isinstance(dr, int) and dr == 0:
            return has_col[dc]
        return jnp.logical_and(has(dr), has_col[dc])

    def device(dr, dc):
        to_band = band + dr
        return (group, to_band // n_sub, col + dc, to_band % n_sub)

    barrier = pltpu.get_barrier_semaphore()

    def member(number):
        return (group, number // (n_sub * n_cols), (number // n_sub) % n_cols, number % n_sub)

    def greet(step, carry):
        pl.semaphore_signal(
            barrier, inc=1, device_id=member((me + step) % members), device_id_type=MESH
        )
        return carry

    lax.fori_loop(1, members, greet, 0)

    loads = []
    for number, (src, dst, at) in enumerate(
        ((elev_hbm, ground, low), (fill_hbm, fill, 0), (edge_hbm, edge, 0))
    ):
        count = src.shape[0]
        for s in range(SUBL):
            pltpu.make_async_copy(
                src.at[:, pl.ds(s * chunk, chunk)],
                dst.at[pl.ds(at, count), s, pl.ds(0, chunk)],
                load_sem.at[number],
            ).start()
        whole = dst.at[pl.ds(at, count), :, pl.ds(0, chunk)]
        loads.append(pltpu.make_async_copy(whole, whole, load_sem.at[number]))
    side_load = pltpu.make_async_copy(side_hbm, side, load_sem.at[3])
    side_load.start()
    adj_load = pltpu.make_async_copy(adj_hbm, adj, load_sem.at[4])
    adj_load.start()

    def outside_rows(at):
        for ref in (ground, first, second, third):
            ref[pl.ds(at, DEPTH)] = jnp.full((DEPTH, SUBL, lanes), unreached, jnp.float32)

    pl.when(jnp.logical_not(has(-1)))(lambda: outside_rows(0))
    pl.when(jnp.logical_not(has(1)))(lambda: outside_rows(high))

    spans = {-1: (0, DEPTH), 0: (low, height), 1: (high, DEPTH)}
    for dc, ref in ((-1, ring_low), (1, ring_high)):
        for dr in (-1, 0, 1):

            def outside_ring(ref=ref, dr=dr):
                at, count = spans[dr]
                ref[:, pl.ds(at, count)] = jnp.full((2, count, 1, TILE), unreached, jnp.float32)

            pl.when(jnp.logical_not(both(dr, dc)))(outside_ring)

    adj_load.wait()
    lane_tile = lax.broadcasted_iota(jnp.int32, (n_tiles, padded), 1)
    linked = jnp.zeros((n_tiles, padded), jnp.float32)
    links = adj[...]
    for k in range(links.shape[1]):
        linked = jnp.where(links[:, k : k + 1] == lane_tile, 1.0, linked)
    own = lax.broadcasted_iota(jnp.int32, (n_tiles, padded), 0) == lane_tile
    linked = jnp.where(own, 1.0, linked)
    one_hop = linked
    if n_tiles < padded:
        one_hop = jnp.concatenate(
            [one_hop, jnp.zeros((padded - n_tiles, padded), jnp.float32)], axis=0
        )
    count = jnp.where(own, 0.0, 1.0)
    reach = linked
    for step in range(ROUNDS):
        count = count + (1.0 - reach)
        if step < ROUNDS - 1:
            reach = jnp.dot(reach, one_hop, preferred_element_type=jnp.float32)
            reach = jnp.where(reach > 0.5, 1.0, 0.0)
    hops[...] = count

    sub_id = lax.broadcasted_iota(jnp.int32, (SUBL, TILE), 0)
    lane_id = lax.broadcasted_iota(jnp.int32, (SUBL, TILE), 1)
    first_cell = jnp.logical_and(sub_id == 0, lane_id == 0)
    last_cell = jnp.logical_and(sub_id == SUBL - 1, lane_id == TILE - 1)
    is_first_col = (col == 0).astype(jnp.int32)
    is_last_col = (col == n_cols - 1).astype(jnp.int32)
    top_mark = jnp.where(band == 0, 1, 2)
    bottom_mark = jnp.where(band == bands - 1, 1, 2)
    right_half = lane_id < HALF

    def ring_of(ref, r):
        left_tile = ref[r, :, 0:TILE]
        right_tile = ref[r, :, chunk - TILE : chunk]
        return jnp.where(
            right_half, pltpu.roll(left_tile, SUBL - 1, 0), pltpu.roll(right_tile, 1, 0)
        )

    side_load.wait()
    for load in loads:
        load.wait()

    def start_row(i):
        height_row = ground[low + i, :, 0:chunk]
        water = height_row + fill[i]
        if i == 0:
            water = jnp.where(edge[0] == top_mark, height_row, water)
        if i == height - 1:
            water = jnp.where(edge[1] == bottom_mark, height_row, water)
        first[low + i, :, 0:chunk] = water
        mark = jnp.where(first_cell, side[0, i] * is_first_col, 0) == 1
        first[low + i, :, 0:TILE] = jnp.where(
            mark, ground[low + i, :, 0:TILE], first[low + i, :, 0:TILE]
        )
        at = chunk - TILE
        mark = jnp.where(last_cell, side[1, i] * is_last_col, 0) == 1
        first[low + i, :, at:chunk] = jnp.where(
            mark, ground[low + i, :, at:chunk], first[low + i, :, at:chunk]
        )
        for number, ref in enumerate((first, ground)):
            ring = ring_of(ref, low + i)
            ring_own[number, i] = ring
            ref[low + i, :, chunk:lanes] = ring

    order = [i for i in range(height) if i < DEPTH or i >= height - DEPTH]
    order += [i for i in range(height) if i not in order]
    for i in order:
        start_row(i)

    pl.semaphore_wait(barrier, members - 1)

    copies = []

    def send(src, dst, dr, dc):
        number = len(copies)
        copy = pltpu.make_async_remote_copy(
            src_ref=src,
            dst_ref=dst,
            send_sem=send_sem.at[number],
            recv_sem=recv_sem.at[number],
            device_id=device(dr, dc),
            device_id_type=MESH,
        )
        pl.when(both(dr, dc))(copy.start)
        copies.append((copy, dr, dc))
        return copy, dr, dc

    def arrive(entry, mirrored):
        copy, dr, dc = entry
        pl.when(both(-dr, -dc) if mirrored else both(dr, dc))(copy.wait_recv)

    def rows_out(ref, dr, extent):
        src = jnp.where(dr < 0, low, high - DEPTH)
        dst = jnp.where(dr < 0, high, 0)
        return send(
            ref.at[pl.ds(src, DEPTH), :, pl.ds(0, extent)],
            ref.at[pl.ds(dst, DEPTH), :, pl.ds(0, extent)],
            dr, 0,
        )

    ring_in = []
    for dc in (-1, 1):
        for dr in (-1, 0, 1):
            at, count = {-1: (0, DEPTH), 0: (0, height), 1: (height - DEPTH, DEPTH)}[dr]
            to, _ = spans[-dr]
            target = ring_high if dc == -1 else ring_low
            part = SUBL - 1 if dc == -1 else 0
            ring_in.append(
                send(
                    ring_own.at[:, pl.ds(at, count), pl.ds(part, 1)],
                    target.at[:, pl.ds(to, count)],
                    dr, dc,
                )
            )
    sides = (near, far)
    row_in = [[rows_out(ref, dr, chunk) for ref in (first, ground)] for dr in sides]

    def relax_rows(src, dst, r, count):
        rows = [src[r - 1 + i] for i in range(count + 2)]
        for i in range(count):
            above, here, below = rows[i : i + 3]
            low3 = jnp.minimum(jnp.minimum(above, below), here)
            least = jnp.minimum(
                low3, jnp.minimum(pltpu.roll(low3, 1, 1), pltpu.roll(low3, lanes - 1, 1))
            )
            value = jnp.maximum(ground[r + i], jnp.minimum(here, least + rise_step))
            if dst is done:
                done[r + i - low] = value[:, 0:chunk]
            else:
                dst[r + i] = value

    def inner(chain):
        for k in range(1, DEPTH + 1):
            for r in range(low + k, high - k, 2):
                relax_rows(chain[k - 1], chain[k], r, 2)

    def outer(chain, dr):
        for k in range(1, DEPTH + 1):
            begin = jnp.where(dr < 0, k, high - k)
            for i in range(0, DEPTH, 2):
                relax_rows(chain[k - 1], chain[k], begin + i, 2)

    def finish_ring(at, count, own_rows):
        for i in range(count):
            r = at + i
            for number, ref in enumerate((first, ground)):
                ring = ring_own[number, i] if own_rows else ring_of(ref, r)
                from_high = jnp.broadcast_to(ring_high[number, r], (SUBL, TILE))
                from_low = jnp.broadcast_to(ring_low[number, r], (SUBL, TILE))
                ring = jnp.where(at_high, from_high, jnp.where(at_low, from_low, ring))
                ref[r, :, chunk:lanes] = ring

    at_high = jnp.logical_and(sub_id == SUBL - 1, right_half)
    at_low = jnp.logical_and(sub_id == 0, jnp.logical_not(right_half))

    for entry in ring_in:
        arrive(entry, True)
    finish_ring(low, height, True)
    chain = (first, ping, pong, ping, second)
    inner(chain)
    row_next = []
    for dr, entries in zip(sides, row_in):
        for entry in entries:
            arrive(entry, False)
        finish_ring(jnp.where(dr < 0, 0, high), DEPTH, False)
        outer(chain, dr)
        row_next.append(rows_out(second, dr, lanes))

    row_in = row_next
    chain = (second, ping, pong, ping, third)
    inner(chain)
    for dr, entry in zip(sides, row_in):
        arrive(entry, False)
        outer(chain, dr)

    first_tile = third[low, :, 0:TILE]
    last_tile = third[low, :, chunk - TILE : chunk]
    for i in range(1, height):
        first_tile = jnp.minimum(first_tile, third[low + i, :, 0:TILE])
        last_tile = jnp.minimum(last_tile, third[low + i, :, chunk - TILE : chunk])
    floor = jnp.minimum(
        jnp.where(first_cell, first_tile, unreached), jnp.where(last_cell, last_tile, unreached)
    )
    for i, counts in ((low, sub == 0), (high - 1, sub == n_sub - 1)):
        skip = jnp.where(counts, -unreached, unreached)
        for j in range(chunk // TILE):
            floor = jnp.minimum(
                floor, jnp.maximum(third[i, :, j * TILE : (j + 1) * TILE], skip)
            )
    floor = jnp.min(floor, axis=(0, 1), keepdims=True)
    tile_id = tile_row * n_cols + col
    mine[...] = jnp.where(
        lax.broadcasted_iota(jnp.int32, (1, padded), 1) == tile_id,
        jnp.broadcast_to(floor, (1, padded)),
        unreached,
    )

    def level_copy(step):
        return pltpu.make_async_remote_copy(
            src_ref=mine,
            dst_ref=gathered.at[members - 1 - step],
            send_sem=level_send,
            recv_sem=level_recv,
            device_id=member((me + step) % members),
            device_id_type=MESH,
        )

    def spread(step, carry):
        level_copy(step).start()
        return carry

    lax.fori_loop(1, members, spread, 0)
    row_in = [rows_out(third, dr, lanes) for dr in (far, near)][::-1]

    chain = (third, ping, pong, ping, done)
    inner(chain)
    for dr, entry in zip(sides, row_in):
        arrive(entry, False)
        outer(chain, dr)

    def seam_of(ref, r):
        ring = ref[r, :, chunk:lanes]
        at_first = jnp.where(right_half, ref[r, :, 0:TILE], ring)
        at_last = jnp.where(right_half, ring, ref[r, :, chunk - TILE : chunk])
        return jnp.where(sub_id == 0, at_first, at_last)

    for r in range(total):
        seam_ground[r] = seam_of(ground, r)

    pltpu.make_async_copy(gathered, gathered, level_recv).wait()
    row = jnp.minimum(mine[...], jnp.min(gathered[...], axis=0))
    count = hops[...]
    best = jnp.full((n_tiles, padded), unreached, jnp.float32)
    for step in range(ROUNDS + 1):
        best = jnp.minimum(
            best, jnp.where(count == float(step), jnp.broadcast_to(row, best.shape), unreached)
        )
        row = row + hop_rise
    level = jnp.min(best, axis=1, keepdims=True)
    levels[...] = jnp.broadcast_to(level + spill_lift, levels.shape)

    def ceiling(row_at, col_at):
        at = jnp.clip(row_at, 0, n_rows - 1) * n_cols + jnp.clip(col_at, 0, n_cols - 1)
        return jnp.broadcast_to(levels[pl.ds(at, 1)], (SUBL, TILE))

    def ceilings(row_at):
        here = ceiling(row_at, col)
        beside = jnp.where(
            at_high, ceiling(row_at, col + 1), jnp.where(at_low, ceiling(row_at, col - 1), here)
        )
        return here, beside

    above, own_row, below = (ceilings((band + dr + n_sub) // n_sub - 1) for dr in (-1, 0, 1))
    beyond = ceilings((band + far + n_sub) // n_sub - 1)

    seam = []
    for r in range(total):
        top = (above if r < low else own_row if r < high else below)[1]
        seam.append(jnp.maximum(seam_ground[r], top))
    for k in range(1, DEPTH + 1):
        later = list(seam)
        for r in range(k, total - k):
            low3 = jnp.minimum(jnp.minimum(seam[r - 1], seam[r + 1]), seam[r])
            least = jnp.minimum(
                low3, jnp.minimum(pltpu.roll(low3, 1, 1), pltpu.roll(low3, TILE - 1, 1))
            )
            later[r] = jnp.maximum(seam_ground[r], jnp.minimum(seam[r], least + rise_step))
        seam = later
    for i in range(height):
        seam_ground[low + i] = seam[low + i]

    def flat(at, count, tops, targets):
        here, beside = tops
        for i in range(count):
            for j in range(lanes // TILE):
                cut = slice(j * TILE, (j + 1) * TILE)
                top = beside if j == lanes // TILE - 1 else here
                value = jnp.maximum(ground[at + i, :, cut], top)
                for target in targets:
                    target[at + i, :, cut] = value

    flat(jnp.where(far < 0, 0, high), DEPTH, beyond, (even,))
    flat(jnp.where(far < 0, low, high - DEPTH - 1), DEPTH + 1, own_row, (even, odd))
    outer((even, odd, even, odd, even), far)

    left_seam = jnp.logical_and(sub_id == 0, lane_id < DEPTH)
    right_seam = jnp.logical_and(sub_id == SUBL - 1, lane_id >= TILE - DEPTH)

    def merge(at, count, is_far):
        for i in range(count):
            r = at + i
            for j in range(chunk // TILE):
                cut = slice(j * TILE, (j + 1) * TILE)
                top = even[r, :, cut] if is_far else jnp.maximum(ground[r, :, cut], own_row[0])
                value = jnp.minimum(done[r - low, :, cut], top)
                if j == 0:
                    value = jnp.where(left_seam, jnp.minimum(value, seam_ground[r]), value)
                if j == chunk // TILE - 1:
                    value = jnp.where(right_seam, jnp.minimum(value, seam_ground[r]), value)
                done[r - low, :, cut] = value

    merge(jnp.where(far < 0, low + DEPTH, low), height - DEPTH, False)
    merge(jnp.where(far < 0, low, high - DEPTH), DEPTH, True)

    for s in range(SUBL):
        pltpu.make_async_copy(
            done.at[:, s], out_hbm.at[:, pl.ds(s * chunk, chunk)], out_sem
        ).start()
    for copy, dr, dc in copies:
        pl.when(both(dr, dc))(copy.wait_send)
    pltpu.make_async_copy(gathered, gathered, level_send).wait()
    pltpu.make_async_copy(done, done, out_sem).wait()


def per_device(sizes, elevation, fill_depth, edge_rows, edge_sides, adjacency):
    height, width = elevation.shape
    chunk = width // SUBL
    total = height + 2 * DEPTH
    members = sizes[1] * sizes[2] * sizes[3]
    n_tiles = adjacency.shape[0]
    padded = -(-n_tiles // TILE) * TILE
    wide = pltpu.VMEM((total, SUBL, chunk + TILE), jnp.float32)
    own = pltpu.VMEM((height, SUBL, chunk), jnp.float32)
    ring = pltpu.VMEM((2, total, 1, TILE), jnp.float32)
    return pl.pallas_call(
        functools.partial(kernel, sizes),
        out_shape=jax.ShapeDtypeStruct((height, width), jnp.float32),
        in_specs=[pl.BlockSpec(memory_space=pltpu.HBM)] * 5,
        out_specs=pl.BlockSpec(memory_space=pl.ANY),
        scratch_shapes=[
            wide, own, wide, wide, wide, wide, wide, own,
            pltpu.VMEM((2, SUBL, chunk), jnp.int32),
            pltpu.SMEM(edge_sides.shape, jnp.int32),
            pltpu.VMEM(adjacency.shape, jnp.int32),
            pltpu.VMEM((2, height, SUBL, TILE), jnp.float32),
            ring, ring,
            pltpu.VMEM((1, padded), jnp.float32),
            pltpu.VMEM((members - 1, 1, padded), jnp.float32),
            pltpu.VMEM((n_tiles, padded), jnp.float32),
            pltpu.VMEM((n_tiles, TILE), jnp.float32),
            wide, wide,
            pltpu.VMEM((total, SUBL, TILE), jnp.float32),
            pltpu.SemaphoreType.DMA((5,)),
            pltpu.SemaphoreType.DMA((14,)),
            pltpu.SemaphoreType.DMA((14,)),
            pltpu.SemaphoreType.DMA,
            pltpu.SemaphoreType.DMA,
            pltpu.SemaphoreType.DMA,
        ],
        compiler_params=pltpu.CompilerParams(
            collective_id=0, has_side_effects=True, vmem_limit_bytes=32 * 1024 * 1024
        ),
    )(elevation, fill_depth, edge_rows, edge_sides, adjacency)


def solution(mesh):
    sizes = tuple(mesh.shape[name] for name in ("groups", "rows", "cols", "sub"))
    placed = (
        P(("groups", "rows", "sub"), "cols"),
        P(("groups", "rows", "sub"), "cols"),
        P("groups", "cols"),
        P("groups", ("rows", "sub")),
        P("groups", None),
    )
    return jax.shard_map(
        functools.partial(per_device, sizes),
        mesh=mesh,
        in_specs=placed,
        out_specs=P(("groups", "rows", "sub"), "cols"),
        check_vma=False,
    )
```

profile of v0, /device:TPU:1, one launch (start us, length us, event | category | flops | bytes accessed | tf_op | source)
XLA Modules:
  0.0 26.8 jit_solution(13030118333912359689)
XLA Ops:
  0.0 0.0 copy-start
  0.0 1.0 %copy-done = f32[16,8192]{1,0:T(8,128)S(1)} copy-done((f32[16,8192]{1,0:T(8,128)S(1)}, f32[16,8192]{1,0:T(8,128)}, u32[]{:S(2)}) %copy-start) | copy-done | bytes 524312
  1.0 0.0 copy-start.1
  1.0 1.0 %copy-done.1 = f32[16,8192]{1,0:T(8,128)S(1)} copy-done((f32[16,8192]{1,0:T(8,128)S(1)}, f32[16,8192]{1,0:T(8,128)}, u32[]{:S(2)}) %copy-start.1) | copy-done | bytes 524312
  2.1 0.0 copy-start.2
  2.1 0.8 %copy-done.2 = s32[2,8192]{1,0:T(2,128)S(1)} copy-done((s32[2,8192]{1,0:T(2,128)S(1)}, s32[2,8192]{1,0:T(2,128)}, u32[]{:S(2)}) %copy-start.2) | copy-done | bytes 65560
  2.9 0.0 copy-start.3
  2.9 0.7 %copy-done.3 = s32[8,6]{1,0:T(8,128)S(1)} copy-done((s32[8,6]{1,0:T(8,128)S(1)}, s32[8,6]{1,0:T(8,128)}, u32[]{:S(2)}) %copy-start.3) | copy-done | bytes 216
  3.6 0.0 copy-start.4
  3.6 0.7 %copy-done.4 = s32[2,16]{1,0:T(2,128)S(1)} copy-done((s32[2,16]{1,0:T(2,128)S(1)}, s32[2,16]{1,0:T(2,128)}, u32[]{:S(2)}) %copy-start.4) | copy-done | bytes 152
  4.3 21.7 %shard_map.55 = f32[16,8192]{1,0:T(8,128)S(1)} custom-call(f32[16,8192]{1,0:T(8,128)S(1)} %copy-done, f32[16,8192]{1,0:T(8,128)S(1)} %copy-done.1, s32[2,8192]{1,0:T(2,128)S(1)} %copy-done.2, s32[2,16]{1,0:T(2,128)S(1)} %copy-done.4, s32[8,6]{1,0:T(8,128)S(1)} %copy-done.3), custom_call_target="tpu_custom_call" | custom-call | tf_op jit(solution)/shard_map/pallas_call | solution.py:442
  26.0 0.8 %copy.7 = f32[16,8192]{1,0:T(8,128)} copy(f32[16,8192]{1,0:T(8,128)S(1)} %shard_map.55) | data formatting | bytes 1048576
Async XLA Ops:
  0.0 1.0 %copy-start = (f32[16,8192]{1,0:T(8,128)S(1)}, f32[16,8192]{1,0:T(8,128)}, u32[]{:S(2)}) copy-start(f32[16,8192]{1,0:T(8,128)} %elev_hbm.1) | copy-start | bytes 1572868
  1.0 1.0 %copy-start.1 = (f32[16,8192]{1,0:T(8,128)S(1)}, f32[16,8192]{1,0:T(8,128)}, u32[]{:S(2)}) copy-start(f32[16,8192]{1,0:T(8,128)} %fill_hbm.1) | copy-start | bytes 1572868
  2.1 0.8 %copy-start.2 = (s32[2,8192]{1,0:T(2,128)S(1)}, s32[2,8192]{1,0:T(2,128)}, u32[]{:S(2)}) copy-start(s32[2,8192]{1,0:T(2,128)} %edge_hbm.1) | copy-start | bytes 196612
  2.9 0.7 %copy-start.3 = (s32[8,6]{1,0:T(8,128)S(1)}, s32[8,6]{1,0:T(8,128)}, u32[]{:S(2)}) copy-start(s32[8,6]{1,0:T(8,128)} %adj_hbm.1) | copy-start | bytes 580
  3.6 0.7 %copy-start.4 = (s32[2,16]{1,0:T(2,128)S(1)}, s32[2,16]{1,0:T(2,128)}, u32[]{:S(2)}) copy-start(s32[2,16]{1,0:T(2,128)} %side_hbm.1) | copy-start | bytes 388
where the time goes:
time: 27.1 us; the launch traced here: 26.8 us
  Pallas kernels  21.7 us (80%)
  local copies, waits for them, and re-layouts  5.08 us (19%)
    pallas_call x1, Pallas kernels, per_device(): pl.pallas_call(functools.partial(kernel, sizes), out_shape=jax.ShapeDtype...  21.7 us
    unnamed x11, local copies, waits for them, and re-layouts  5.08 us

commit v1 on v0

--- a/solution.py
+++ b/solution.py
@@ -465,7 +465,7 @@
             pltpu.SemaphoreType.DMA,
         ],
         compiler_params=pltpu.CompilerParams(
-            collective_id=0, has_side_effects=True, vmem_limit_bytes=32 * 1024 * 1024
+            collective_id=0, has_side_effects=True, vmem_limit_bytes=66 * 1000 * 1000
         ),
     )(elevation, fill_depth, edge_rows, edge_sides, adjacency)
 

time: 27.1 us -> 24.2 us (0.89)
  local copies, waits for them, and re-layouts: 5.08 us -> 1.87 us
  Pallas kernels: 21.7 us -> 22.1 us
    unnamed x11 -> x1, local copies, waits for them, and re-layouts: 5.08 us -> 1.87 us
    pallas_call x1, Pallas kernels: 21.7 us -> 22.1 us  [per_device(): pl.pallas_call(functools.partial(kernel, sizes), out_shape=jax.ShapeDtype...]
where the time goes in v1:
time: 24.2 us; the launch traced here: 24 us
  Pallas kernels  22.1 us (91%)
  local copies, waits for them, and re-layouts  1.87 us (8%)
    pallas_call x1, Pallas kernels, per_device(): pl.pallas_call(functools.partial(kernel, sizes), out_shape=jax.ShapeDtype...  22.1 us
    unnamed x1, local copies, waits for them, and re-layouts  1.87 us

profile of v1, /device:TPU:1, one launch (start us, length us, event | category | flops | bytes accessed | tf_op | source)
XLA Modules:
  0.0 24.0 jit_solution(1910615599946612840)
XLA Ops:
  0.0 22.1 %shard_map.55 = f32[16,8192]{1,0:T(8,128)} custom-call(f32[16,8192]{1,0:T(8,128)} %elev_hbm.1, f32[16,8192]{1,0:T(8,128)} %fill_hbm.1, s32[2,8192]{1,0:T(2,128)} %edge_hbm.1, s32[2,16]{1,0:T(2,128)} %side_hbm.1, s32[8,6]{1,0:T(8,128)} %adj_hbm.1), custom_call_target="tpu_custom_call" | custom-call | tf_op jit(solution)/shard_map/pallas_call | solution.py:442
  22.1 1.9 %copy.7 = f32[16,8192]{1,0:T(8,128)} copy(f32[16,8192]{1,0:T(8,128)} %shard_map.55) | data formatting | bytes 1048576

commit v2 on v0

v2 whole, which is shorter than its diff:
```python
import functools

import jax
import jax.numpy as jnp
from jax import lax
from jax.experimental import pallas as pl
from jax.experimental.pallas import tpu as pltpu
from jax.sharding import PartitionSpec as P

PASSES = 8
FINAL = 4
ROUNDS = 4

unreached = 1000000000.0
rise_step = 0.01
hop_rise = 0.05
spill_lift = 3.0

DEEP = PASSES + FINAL
CUTS = (0, 4, 6, 8, 10, 12)
SUBL = 8
TILE = 128
HALF = TILE // 2
MESH = pl.DeviceIdType.MESH


def kernel(
    sizes, elev_hbm, fill_hbm, edge_hbm, side_hbm, adj_hbm, out,
    elev, fill, far_elev, ground, first, ping, pong, walks,
    edge, side, adj, ring_own, ring_low, ring_high, column_floor,
    mine, gathered, hops, levels, seam_ground,
    load_sem, send_sem, recv_sem, level_send, level_recv,
):
    n_groups, n_rows, n_cols, n_sub = sizes
    tiles = edge_hbm.shape[0] // (2 * SUBL)
    chunk = tiles * TILE
    lanes = chunk + TILE
    half_rows = SUBL * tiles * SUBL
    halves = elev_hbm.shape[0] // half_rows
    height = halves * SUBL
    n_tiles = adj.shape[0]
    padded = mine.shape[1]
    members = n_rows * n_cols * n_sub

    group = lax.axis_index("groups")
    tile_row = lax.axis_index("rows")
    col = lax.axis_index("cols")
    sub = lax.axis_index("sub")
    band = tile_row * n_sub + sub
    bands = n_rows * n_sub
    me = (tile_row * n_cols + col) * n_sub + sub

    near = 1 - 2 * sub
    far = -near

    def row_of(i):
        return jnp.where(sub == 0, i, height - 1 - i)

    def slot(i):
        if i < 0:
            return -1 - i
        if i < height:
            return DEEP + i
        return 2 * DEEP + 2 * height - 1 - i

    def has(dr):
        return jnp.logical_and(band + dr >= 0, band + dr < bands)

    has_col = {-1: col > 0, 1: col < n_cols - 1}

    def both(side_of, dc):
        there = {0: None, 1: has(far), 2: None}[side_of]
        if dc == 0:
            return there
        return has_col[dc] if there is None else jnp.logical_and(there, has_col[dc])

    def device(side_of, dc):
        to_band = band + {0: 0, 1: far, 2: near}[side_of]
        return (group, to_band // n_sub, col + dc, to_band % n_sub)

    def when(condition, action):
        if condition is None:
            action()
        else:
            pl.when(condition)(action)

    barrier = pltpu.get_barrier_semaphore()

    def member(number):
        return (group, number // (n_sub * n_cols), (number // n_sub) % n_cols, number % n_sub)

    def greet(step, carry):
        pl.semaphore_signal(
            barrier, inc=1, device_id=member((me + step) % members), device_id_type=MESH
        )
        return carry

    loads = []
    for part in range(halves):
        half = row_of(part * SUBL) // SUBL
        at = pl.ds(pl.multiple_of(half * half_rows, half_rows), half_rows)
        pair = []
        for number, (src, dst) in enumerate(((elev_hbm, elev), (fill_hbm, fill))):
            copy = pltpu.make_async_copy(src.at[at], dst.at[at], load_sem.at[2 * part + number])
            copy.start()
            pair.append(copy)
        loads.append(pair)
    spare = 2 * halves
    side_load = pltpu.make_async_copy(side_hbm, side, load_sem.at[spare])
    side_load.start()
    edge_load = pltpu.make_async_copy(edge_hbm, edge, load_sem.at[spare + 1])
    edge_load.start()
    adj_load = pltpu.make_async_copy(adj_hbm, adj, load_sem.at[spare + 2])
    adj_load.start()
    lax.fori_loop(1, members, greet, 0)

    def outside_rows():
        for ref in (ground, first):
            ref[0:DEEP] = jnp.full((DEEP, SUBL, lanes), unreached, jnp.float32)
        far_elev[...] = jnp.full(far_elev.shape, unreached, jnp.float32)

    pl.when(jnp.logical_not(has(far)))(outside_rows)

    spans = {0: (DEEP, height), 1: (0, DEEP), 2: (DEEP + height, DEEP)}
    for dc, ref in ((-1, ring_low), (1, ring_high)):
        for side_of in (0, 1, 2):

            def outside_ring(ref=ref, side_of=side_of):
                at, count = spans[side_of]
                ref[:, at : at + count] = jnp.full((2, count, 1, TILE), unreached, jnp.float32)

            pl.when(jnp.logical_not(both(side_of, dc)))(outside_ring)
    column_floor[...] = jnp.full(column_floor.shape, unreached, jnp.float32)

    sub_id = lax.broadcasted_iota(jnp.int32, (SUBL, TILE), 0)
    lane_id = lax.broadcasted_iota(jnp.int32, (SUBL, TILE), 1)
    first_cell = jnp.logical_and(sub_id == 0, lane_id == 0)
    last_cell = jnp.logical_and(sub_id == SUBL - 1, lane_id == TILE - 1)
    is_first_col = (col == 0).astype(jnp.int32)
    is_last_col = (col == n_cols - 1).astype(jnp.int32)
    at_slab_edge = jnp.where(has(far), 2, 1)
    right_half = lane_id < HALF
    at_high = jnp.logical_and(sub_id == SUBL - 1, right_half)
    at_low = jnp.logical_and(sub_id == 0, jnp.logical_not(right_half))

    def ring_of(ref, at):
        left_tile = ref[at, :, 0:TILE]
        right_tile = ref[at, :, chunk - TILE : chunk]
        return jnp.where(
            right_half, pltpu.roll(left_tile, SUBL - 1, 0), pltpu.roll(right_tile, 1, 0)
        )

    def piece(i, v):
        row = row_of(i)
        at = (row // SUBL) * half_rows + v * SUBL + row % SUBL
        return pl.ds(at, SUBL, stride=tiles * SUBL), slice(None)

    edge_side = jnp.where(far < 0, 0, 1)

    def start_row(i, columns):
        row = row_of(i)
        for v in columns:
            cut = slice(v * TILE, (v + 1) * TILE)
            here = elev[piece(i, v)]
            water = here + fill[piece(i, v)]
            if i == 0:
                marks = edge[pl.ds(2 * v + edge_side, SUBL, stride=2 * tiles), :]
                water = jnp.where(marks == at_slab_edge, here, water)
            if v == 0:
                mark = jnp.where(first_cell, side[0, row] * is_first_col, 0) == 1
                water = jnp.where(mark, here, water)
            if v == tiles - 1:
                mark = jnp.where(last_cell, side[1, row] * is_last_col, 0) == 1
                water = jnp.where(mark, here, water)
            ground[slot(i), :, cut] = here
            first[slot(i), :, cut] = water

    def start_ring(i):
        for number, ref in enumerate((first, ground)):
            ring_own[number, i] = ring_of(ref, slot(i))

    copies = []

    def send(src, dst, side_of, dc):
        number = len(copies)
        copy = pltpu.make_async_remote_copy(
            src_ref=src,
            dst_ref=dst,
            send_sem=send_sem.at[number],
            recv_sem=recv_sem.at[number],
            device_id=device(side_of, dc),
            device_id_type=MESH,
        )
        when(both(side_of, dc), copy.start)
        copies.append((copy, side_of, dc))
        return copy, side_of, dc

    def arrive(entry):
        copy, side_of, dc = entry
        when(both(side_of, -dc), copy.wait_recv)

    def send_rows(ref, side_of, i, count, to):
        return send(
            ref.at[pl.ds(slot(i), count), :, pl.ds(0, chunk)],
            ref.at[pl.ds(to, count), :, pl.ds(0, chunk)],
            side_of, 0,
        )

    def send_ring(side_of, i, count, to):
        sent = []
        for dc in (-1, 1):
            target = ring_high if dc == -1 else ring_low
            part = SUBL - 1 if dc == -1 else 0
            sent.append(
                send(
                    ring_own.at[:, pl.ds(i, count), pl.ds(part, 1)],
                    target.at[:, pl.ds(to, count)],
                    side_of, dc,
                )
            )
        return sent

    pl.semaphore_wait(barrier, members - 1)
    far_half = row_of(0) // SUBL
    at = pl.ds(pl.multiple_of(far_half * half_rows, half_rows), half_rows)
    far_ground = send(elev_hbm.at[at], far_elev, 1, 0)
    side_load.wait()
    edge_load.wait()
    for pair in loads:
        for load in pair:
            load.wait()
    for i in range(height):
        start_row(i, (0, tiles - 1))
        start_ring(i)
    own_ring = send_ring(0, 0, height, DEEP)
    near_ring = send_ring(2, height - DEEP, DEEP, DEEP + height)
    far_ring = send_ring(1, 0, DEEP, 0)
    between = range(1, tiles - 1)
    far_rows = []
    for begin, end in zip(CUTS[:-1], CUTS[1:]):
        for i in range(begin, end):
            if not SUBL + 2 <= i < DEEP - 1:
                start_row(i, between)
        entries = []
        if begin == SUBL:
            for i in range(end, DEEP - 1):
                start_row(i, between)
            entries.append(send_rows(ground, 1, SUBL, DEEP - 1 - SUBL, SUBL))
        entries.append(send_rows(first, 1, begin, end - begin, begin))
        far_rows.append(entries)
    far_rows[0].append(far_ground)
    for i in range(DEEP, height):
        start_row(i, between)
    near_rows = [
        send_rows(ref, 2, height - DEEP, DEEP, DEEP + height) for ref in (first, ground)
    ]

    adj_load.wait()
    lane_tile = lax.broadcasted_iota(jnp.int32, (n_tiles, padded), 1)
    linked = jnp.zeros((n_tiles, padded), jnp.float32)
    links = adj[...]
    for k in range(links.shape[1]):
        linked = jnp.where(links[:, k : k + 1] == lane_tile, 1.0, linked)
    own = lax.broadcasted_iota(jnp.int32, (n_tiles, padded), 0) == lane_tile
    linked = jnp.where(own, 1.0, linked)
    one_hop = linked
    if n_tiles < padded:
        one_hop = jnp.concatenate(
            [one_hop, jnp.zeros((padded - n_tiles, padded), jnp.float32)], axis=0
        )
    count = jnp.where(own, 0.0, 1.0)
    reach = linked
    for step in range(ROUNDS):
        count = count + (1.0 - reach)
        if step < ROUNDS - 1:
            reach = jnp.dot(reach, one_hop, preferred_element_type=jnp.float32)
            reach = jnp.where(reach > 0.5, 1.0, 0.0)
    hops[...] = count

    def finish_ring(i, own_row):
        at = slot(i)
        for number, ref in enumerate((first, ground)):
            ring = ring_own[number, i] if own_row else ring_of(ref, at)
            from_high = jnp.broadcast_to(ring_high[number, at], (SUBL, TILE))
            from_low = jnp.broadcast_to(ring_low[number, at], (SUBL, TILE))
            ring = jnp.where(at_high, from_high, jnp.where(at_low, from_low, ring))
            ref[at, :, chunk:lanes] = ring

    def state(k):
        return first if k == 0 else ping if k % 2 else pong

    def least_of(low):
        return jnp.minimum(
            low, jnp.minimum(pltpu.roll(low, 1, 1), pltpu.roll(low, lanes - 1, 1))
        )

    def relax(k, begin, end):
        src, dst = state(k - 1), state(k)
        for at in range(begin, end, 2):
            count = min(2, end - at)
            rows = [src[slot(at - 1 + j)] for j in range(count + 2)]
            for j in range(count):
                above, here, below = rows[j : j + 3]
                least = least_of(jnp.minimum(jnp.minimum(above, below), here))
                value = jnp.maximum(ground[slot(at + j)], jnp.minimum(here, least + rise_step))
                dst[slot(at + j)] = value
                if k == PASSES and 0 <= at + j < height:
                    column_floor[0] = jnp.minimum(column_floor[0], value[:, 0:TILE])
                    column_floor[1] = jnp.minimum(column_floor[1], value[:, chunk - TILE : chunk])

    for entry in own_ring:
        arrive(entry)
    for i in range(height):
        finish_ring(i, True)
    for k in range(1, height // 2):
        relax(k, k, height - k)

    for entry in near_rows + near_ring:
        arrive(entry)
    for i in range(height, height + DEEP):
        finish_ring(i, False)
    for k in range(1, PASSES + 1):
        relax(k, height - k, height + PASSES - k)

    def strip(number, passes):
        for k in passes:
            relax(k, k - CUTS[number + 1], k - CUTS[number])

    def open_strip(number):
        for entry in far_rows[number]:
            arrive(entry)
        for i in range(-CUTS[number + 1], -CUTS[number]):
            finish_ring(i, False)

    for entry in far_ring + far_rows[0]:
        arrive(entry)
    for i in range(SUBL):
        at = jnp.where(sub == 0, SUBL - 1 - i, i)
        for v in range(tiles):
            ground[slot(-1 - i), :, v * TILE : (v + 1) * TILE] = far_elev[
                pl.ds(at + v * SUBL, SUBL, stride=tiles * SUBL), :
            ]
    for i in range(-CUTS[1], 0):
        finish_ring(i, False)
    strip(0, range(1, PASSES + 1))
    for k in range(1, DEEP + 1):
        relax(k, k if k > PASSES else height + PASSES - k, height + DEEP - k)
    for number in (1, 2):
        open_strip(number)
        strip(number, range(1, PASSES + 1))

    floor = jnp.minimum(
        jnp.where(first_cell, column_floor[0], unreached),
        jnp.where(last_cell, column_floor[1], unreached),
    )
    for v in range(tiles):
        floor = jnp.minimum(floor, state(PASSES)[slot(0), :, v * TILE : (v + 1) * TILE])
    floor = jnp.min(floor, axis=(0, 1), keepdims=True)
    tile_id = tile_row * n_cols + col
    mine[...] = jnp.where(
        lax.broadcasted_iota(jnp.int32, (1, padded), 1) == tile_id,
        jnp.broadcast_to(floor, (1, padded)),
        unreached,
    )

    def level_copy(step):
        return pltpu.make_async_remote_copy(
            src_ref=mine,
            dst_ref=gathered.at[members - 1 - step],
            send_sem=level_send,
            recv_sem=level_recv,
            device_id=member((me + step) % members),
            device_id_type=MESH,
        )

    def spread(step, carry):
        level_copy(step).start()
        return carry

    lax.fori_loop(1, members, spread, 0)

    for k in range(PASSES + 1, DEEP + 1):
        relax(k, k - PASSES, k)

    def walk_at(n, r):
        return n * (n - 1) // 2 + r

    entry_row = ground[slot(-1)]
    entry_ring = jnp.where(jnp.logical_or(at_high, at_low), unreached, entry_row[:, chunk:lanes])
    before = [jnp.concatenate([entry_row[:, 0:chunk], entry_ring], axis=1)]
    for n in range(1, FINAL + 1):
        for r in range(n):
            low = None
            for q in range(max(r - 1, 0), min(r + 2, len(before))):
                row = before[q]
                low = row if low is None else jnp.minimum(low, row)
            walks[walk_at(n, r)] = jnp.maximum(ground[slot(r)], least_of(low) + rise_step)
        before = [walks[walk_at(n, r)] for r in range(n)]

    def seam_of(ref, at):
        ring = ref[at, :, chunk:lanes]
        at_first = jnp.where(right_half, ref[at, :, 0:TILE], ring)
        at_last = jnp.where(right_half, ring, ref[at, :, chunk - TILE : chunk])
        return jnp.where(sub_id == 0, at_first, at_last)

    seam_rows = list(range(-FINAL, height + FINAL))
    for j, i in enumerate(seam_rows):
        seam_ground[j] = seam_of(ground, slot(i))

    for number in (3, 4):
        open_strip(number)
        strip(number, range(1, DEEP + 1))

    pltpu.make_async_copy(gathered, gathered, level_recv).wait()
    row = jnp.minimum(mine[...], jnp.min(gathered[...], axis=0))
    count = hops[...]
    best = jnp.full((n_tiles, padded), unreached, jnp.float32)
    for step in range(ROUNDS + 1):
        best = jnp.minimum(
            best, jnp.where(count == float(step), jnp.broadcast_to(row, best.shape), unreached)
        )
        row = row + hop_rise
    level = jnp.min(best, axis=1, keepdims=True)
    levels[...] = jnp.broadcast_to(level + spill_lift, levels.shape)

    def ceiling(row_at, col_at):
        at = jnp.clip(row_at, 0, n_rows - 1) * n_cols + jnp.clip(col_at, 0, n_cols - 1)
        return jnp.broadcast_to(levels[pl.ds(at, 1)], (SUBL, TILE))

    def ceilings(row_at):
        here = ceiling(row_at, col)
        beside = jnp.where(
            at_high, ceiling(row_at, col + 1), jnp.where(at_low, ceiling(row_at, col - 1), here)
        )
        return here, beside

    own_top, own_beside = ceilings(tile_row)
    far_top, far_beside = ceilings(tile_row + far)

    seam = []
    for j, i in enumerate(seam_rows):
        seam.append(jnp.maximum(seam_ground[j], far_beside if i < 0 else own_beside))
    for k in range(1, FINAL + 1):
        later = list(seam)
        for j in range(k, len(seam) - k):
            low = jnp.minimum(jnp.minimum(seam[j - 1], seam[j + 1]), seam[j])
            least = jnp.minimum(low, jnp.minimum(pltpu.roll(low, 1, 1), pltpu.roll(low, TILE - 1, 1)))
            later[j] = jnp.maximum(seam_ground[j], jnp.minimum(seam[j], least + rise_step))
        seam = later

    left_seam = jnp.logical_and(sub_id == 0, lane_id < FINAL)
    right_seam = jnp.logical_and(sub_id == SUBL - 1, lane_id >= TILE - FINAL)
    tops = []
    for n in range(1, FINAL + 1):
        far_top = far_top + rise_step
        tops.append(far_top)
    for i in range(height):
        for v in range(tiles):
            cut = slice(v * TILE, (v + 1) * TILE)
            top = jnp.maximum(ground[slot(i), :, cut], own_top)
            for n in range(i + 1, FINAL + 1):
                top = jnp.minimum(top, jnp.maximum(walks[walk_at(n, i), :, cut], tops[n - 1]))
            value = jnp.minimum(state(DEEP)[slot(i), :, cut], top)
            if v == 0:
                value = jnp.where(left_seam, jnp.minimum(value, seam[i + FINAL]), value)
            if v == tiles - 1:
                value = jnp.where(right_seam, jnp.minimum(value, seam[i + FINAL]), value)
            out[piece(i, v)] = value

    for copy, side_of, dc in copies:
        when(both(side_of, dc), copy.wait_send)
    pltpu.make_async_copy(gathered, gathered, level_send).wait()


def per_device(sizes, elevation, fill_depth, edge_rows, edge_sides, adjacency):
    height, width = elevation.shape
    chunk = width // SUBL
    tiles = width // TILE
    total = height + 2 * DEEP
    members = sizes[1] * sizes[2] * sizes[3]
    n_tiles = adjacency.shape[0]
    padded = -(-n_tiles // TILE) * TILE
    flat = (height * tiles, TILE)

    def tiled(array):
        blocks = array.reshape(height // SUBL, SUBL, tiles, TILE)
        return blocks.transpose(0, 2, 1, 3).reshape(flat)

    wide = pltpu.VMEM((total, SUBL, chunk + TILE), jnp.float32)
    whole = pltpu.VMEM(flat, jnp.float32)
    ring = pltpu.VMEM((2, total, 1, TILE), jnp.float32)
    marks = edge_rows.reshape(2, tiles, TILE).transpose(1, 0, 2).reshape(2 * tiles, TILE)
    operands = (tiled(elevation), tiled(fill_depth), marks, edge_sides, adjacency)
    filled = pl.pallas_call(
        functools.partial(kernel, sizes),
        out_shape=pltpu.VMEM(flat, jnp.float32),
        in_specs=[pl.BlockSpec(memory_space=pltpu.HBM)] * 5,
        out_specs=pl.BlockSpec(memory_space=pltpu.VMEM),
        scratch_shapes=[
            whole, whole,
            pltpu.VMEM((SUBL * tiles, TILE), jnp.float32),
            wide, wide, wide, wide,
            pltpu.VMEM((FINAL * (FINAL + 1) // 2, SUBL, chunk + TILE), jnp.float32),
            pltpu.VMEM((2 * tiles, TILE), jnp.int32),
            pltpu.SMEM(edge_sides.shape, jnp.int32),
            pltpu.VMEM(adjacency.shape, jnp.int32),
            pltpu.VMEM((2, height, SUBL, TILE), jnp.float32),
            ring, ring,
            pltpu.VMEM((2, SUBL, TILE), jnp.float32),
            pltpu.VMEM((1, padded), jnp.float32),
            pltpu.VMEM((members - 1, 1, padded), jnp.float32),
            pltpu.VMEM((n_tiles, padded), jnp.float32),
            pltpu.VMEM((n_tiles, TILE), jnp.float32),
            pltpu.VMEM((height + 2 * FINAL, SUBL, TILE), jnp.float32),
            pltpu.SemaphoreType.DMA((2 * (height // SUBL) + 3,)),
            pltpu.SemaphoreType.DMA((15,)),
            pltpu.SemaphoreType.DMA((15,)),
            pltpu.SemaphoreType.DMA,
            pltpu.SemaphoreType.DMA,
        ],
        compiler_params=pltpu.CompilerParams(
            collective_id=0, has_side_effects=True, vmem_limit_bytes=32 * 1024 * 1024
        ),
    )(*(pltpu.with_memory_space_constraint(each, pltpu.HBM) for each in operands))
    blocks = filled.reshape(height // SUBL, tiles, SUBL, TILE)
    return blocks.transpose(0, 2, 1, 3).reshape(height, width)


def solution(mesh):
    sizes = tuple(mesh.shape[name] for name in ("groups", "rows", "cols", "sub"))
    placed = (
        P(("groups", "rows", "sub"), "cols"),
        P(("groups", "rows", "sub"), "cols"),
        P("groups", "cols"),
        P("groups", ("rows", "sub")),
        P("groups", None),
    )
    return jax.shard_map(
        functools.partial(per_device, sizes),
        mesh=mesh,
        in_specs=placed,
        out_specs=P(("groups", "rows", "sub"), "cols"),
        check_vma=False,
    )
```

time: 27.1 us -> 22.2 us (0.82)
  local copies, waits for them, and re-layouts: 5.08 us -> 0.8 us
  Pallas kernels: 21.7 us -> 21.3 us
    unnamed x11 -> x1, local copies, waits for them, and re-layouts: 5.08 us -> 0.8 us
    pallas_call x1, Pallas kernels: 21.7 us -> 21.3 us  [per_device(): pl.pallas_call(functools.partial(kernel, sizes), out_shape=pltpu.VMEM(fla...]
where the time goes in v2:
time: 22.2 us; the launch traced here: 22.1 us
  Pallas kernels  21.3 us (96%)
  local copies, waits for them, and re-layouts  0.8 us (4%)
    pallas_call x1, Pallas kernels, per_device(): pl.pallas_call(functools.partial(kernel, sizes), out_shape=pltpu.VMEM(fla...  21.3 us
    unnamed x1, local copies, waits for them, and re-layouts  0.8 us

profile of v2, /device:TPU:1, one launch (start us, length us, event | category | flops | bytes accessed | tf_op | source)
XLA Modules:
  0.0 22.1 jit_solution(17154743887031907059)
XLA Ops:
  0.0 21.3 %shard_map.55 = f32[1024,128]{1,0:T(8,128)S(1)} custom-call(f32[1024,128]{1,0:T(8,128)} %bitcast.21, f32[1024,128]{1,0:T(8,128)} %bitcast.22, s32[128,128]{1,0:T(8,128)} %bitcast.23, s32[2,16]{1,0:T(2,128)} %side_hbm.1, s32[8,6]{1,0:T(8,128)} %adj_hbm.1), custom_call_target="tpu_custom_call" | custom-call | tf_op jit(solution)/shard_map/pallas_call | solution.py:494
  21.3 0.8 %copy.8 = f32[16,8192]{1,0:T(8,128)} copy(f32[16,8192]{1,0:T(8,128)S(1)} %bitcast.20) | data formatting | bytes 1048576

commit v3 on v2

--- a/solution.py
+++ b/solution.py
@@ -28,13 +28,14 @@
     sizes, elev_hbm, fill_hbm, edge_hbm, side_hbm, adj_hbm, out,
     elev, fill, far_elev, ground, first, ping, pong, walks,
     edge, side, adj, ring_own, ring_low, ring_high, column_floor,
-    mine, gathered, hops, levels, seam_ground,
+    mine, gathered, hops, levels, seam_ground, seam_sides, split, join,
     load_sem, send_sem, recv_sem, level_send, level_recv,
 ):
     n_groups, n_rows, n_cols, n_sub = sizes
     tiles = edge_hbm.shape[0] // (2 * SUBL)
     chunk = tiles * TILE
-    lanes = chunk + TILE
+    pairs = tiles // 2
+    lanes = chunk + 2 * TILE
     half_rows = SUBL * tiles * SUBL
     halves = elev_hbm.shape[0] // half_rows
     height = halves * SUBL
@@ -90,11 +91,13 @@
         return (group, number // (n_sub * n_cols), (number // n_sub) % n_cols, number % n_sub)
 
     def greet(step, carry):
+        apart = step
         pl.semaphore_signal(
-            barrier, inc=1, device_id=member((me + step) % members), device_id_type=MESH
+            barrier, inc=1, device_id=member((me + apart) % members), device_id_type=MESH
         )
         return carry
 
+    lax.fori_loop(1, members, greet, 0)
     loads = []
     for part in range(halves):
         half = row_of(part * SUBL) // SUBL
@@ -112,7 +115,6 @@
     edge_load.start()
     adj_load = pltpu.make_async_copy(adj_hbm, adj, load_sem.at[spare + 2])
     adj_load.start()
-    lax.fori_loop(1, members, greet, 0)
 
     def outside_rows():
         for ref in (ground, first):
@@ -127,7 +129,7 @@
 
             def outside_ring(ref=ref, side_of=side_of):
                 at, count = spans[side_of]
-                ref[:, at : at + count] = jnp.full((2, count, 1, TILE), unreached, jnp.float32)
+                ref[:, at : at + count] = jnp.full((4, count, 1, TILE), unreached, jnp.float32)
 
             pl.when(jnp.logical_not(both(side_of, dc)))(outside_ring)
     column_floor[...] = jnp.full(column_floor.shape, unreached, jnp.float32)
@@ -143,41 +145,89 @@
     at_high = jnp.logical_and(sub_id == SUBL - 1, right_half)
     at_low = jnp.logical_and(sub_id == 0, jnp.logical_not(right_half))
 
-    def ring_of(ref, at):
-        left_tile = ref[at, :, 0:TILE]
-        right_tile = ref[at, :, chunk - TILE : chunk]
+    near_id = lax.broadcasted_iota(jnp.int32, (2 * TILE, 2 * TILE), 0)
+    pair_id = lax.broadcasted_iota(jnp.int32, (2 * TILE, 2 * TILE), 1)
+    split[...] = (near_id == 2 * (pair_id % TILE) + pair_id // TILE).astype(jnp.bfloat16)
+    join[...] = (pair_id == 2 * (near_id % TILE) + near_id // TILE).astype(jnp.bfloat16)
+
+    def shuffled(blocks, order):
+        whole = jnp.concatenate([jnp.concatenate(block, axis=1) for block in blocks], axis=0)
+        total = None
+        for term in range(3):
+            part = whole.astype(jnp.bfloat16)
+            whole = whole - part.astype(jnp.float32)
+            moved = jnp.dot(part, order[...], preferred_element_type=jnp.float32)
+            total = moved if total is None else total + moved
+        return [
+            (total[SUBL * b : SUBL * (b + 1), 0:TILE], total[SUBL * b : SUBL * (b + 1), TILE : 2 * TILE])
+            for b in range(len(blocks))
+        ]
+
+    def tile_of(ref, at, v):
+        return ref[at, :, v * TILE : (v + 1) * TILE]
+
+    def put_tile(ref, at, v, value):
+        ref[at, :, v * TILE : (v + 1) * TILE] = value
+
+    def ring_of(ref, at, p):
         return jnp.where(
-            right_half, pltpu.roll(left_tile, SUBL - 1, 0), pltpu.roll(right_tile, 1, 0)
-        )
-
-    def piece(i, v):
-        row = row_of(i)
-        at = (row // SUBL) * half_rows + v * SUBL + row % SUBL
-        return pl.ds(at, SUBL, stride=tiles * SUBL), slice(None)
-
-    edge_side = jnp.where(far < 0, 0, 1)
-
-    def start_row(i, columns):
-        row = row_of(i)
-        for v in columns:
-            cut = slice(v * TILE, (v + 1) * TILE)
-            here = elev[piece(i, v)]
-            water = here + fill[piece(i, v)]
-            if i == 0:
-                marks = edge[pl.ds(2 * v + edge_side, SUBL, stride=2 * tiles), :]
-                water = jnp.where(marks == at_slab_edge, here, water)
-            if v == 0:
-                mark = jnp.where(first_cell, side[0, row] * is_first_col, 0) == 1
-                water = jnp.where(mark, here, water)
-            if v == tiles - 1:
-                mark = jnp.where(last_cell, side[1, row] * is_last_col, 0) == 1
-                water = jnp.where(mark, here, water)
-            ground[slot(i), :, cut] = here
-            first[slot(i), :, cut] = water
+            right_half,
+            pltpu.roll(tile_of(ref, at, p), SUBL - 1, 0),
+            pltpu.roll(tile_of(ref, at, tiles - 2 + p), 1, 0),
+        )
+
+    def turned(rows):
+        rows = list(rows)
+        for step in (4, 2, 1):
+            stays = sub_id % (2 * step) < step
+            for at in range(SUBL):
+                if at % (2 * step) < step:
+                    one, two = rows[at], rows[at + step]
+                    rows[at] = jnp.where(stays, one, pltpu.roll(two, step, 0))
+                    rows[at + step] = jnp.where(stays, pltpu.roll(one, SUBL - step, 0), two)
+        return rows
+
+    def natural(half, s, v):
+        at = half * half_rows + (s * tiles + v) * SUBL
+        return slice(at, at + SUBL)
+
+    def by_side(action):
+        pl.when(sub == 0)(lambda: action(False))
+        pl.when(sub == 1)(lambda: action(True))
+
+    def start_rows(part, groups):
+        def action(flip):
+            half = halves - 1 - part if flip else part
+            for g in groups:
+                here, water = {}, {}
+                for v in (2 * g, 2 * g + 1):
+                    rock = [elev[natural(half, s, v), :] for s in range(SUBL)]
+                    deep = [rock[s] + fill[natural(half, s, v), :] for s in range(SUBL)]
+                    here[v], water[v] = turned(rock), turned(deep)
+                    for r in range(SUBL):
+                        row = half * SUBL + r
+                        if row == (height - 1 if flip else 0):
+                            marks = edge[pl.ds(2 * v + flip, SUBL, stride=2 * tiles), :]
+                            water[v][r] = jnp.where(marks == at_slab_edge, here[v][r], water[v][r])
+                        if v == 0:
+                            mark = jnp.where(first_cell, side[0, row] * is_first_col, 0) == 1
+                            water[v][r] = jnp.where(mark, here[v][r], water[v][r])
+                        if v == tiles - 1:
+                            mark = jnp.where(last_cell, side[1, row] * is_last_col, 0) == 1
+                            water[v][r] = jnp.where(mark, here[v][r], water[v][r])
+                for ref, array in ((ground, here), (first, water)):
+                    moved = shuffled([(array[2 * g][r], array[2 * g + 1][r]) for r in range(SUBL)], split)
+                    for r, pair in enumerate(moved):
+                        row = half * SUBL + r
+                        for p in (0, 1):
+                            put_tile(ref, slot(height - 1 - row if flip else row), 2 * g + p, pair[p])
+
+        by_side(action)
 
     def start_ring(i):
         for number, ref in enumerate((first, ground)):
-            ring_own[number, i] = ring_of(ref, slot(i))
+            for p in (0, 1):
+                ring_own[2 * number + p, i] = ring_of(ref, slot(i), p)
 
     copies = []
 
@@ -229,28 +279,23 @@
     for pair in loads:
         for load in pair:
             load.wait()
+    for part in range(halves):
+        start_rows(part, (0, pairs - 1))
     for i in range(height):
-        start_row(i, (0, tiles - 1))
         start_ring(i)
     own_ring = send_ring(0, 0, height, DEEP)
     near_ring = send_ring(2, height - DEEP, DEEP, DEEP + height)
     far_ring = send_ring(1, 0, DEEP, 0)
-    between = range(1, tiles - 1)
     far_rows = []
-    for begin, end in zip(CUTS[:-1], CUTS[1:]):
-        for i in range(begin, end):
-            if not SUBL + 2 <= i < DEEP - 1:
-                start_row(i, between)
-        entries = []
-        if begin == SUBL:
-            for i in range(end, DEEP - 1):
-                start_row(i, between)
-            entries.append(send_rows(ground, 1, SUBL, DEEP - 1 - SUBL, SUBL))
-        entries.append(send_rows(first, 1, begin, end - begin, begin))
-        far_rows.append(entries)
-    far_rows[0].append(far_ground)
-    for i in range(DEEP, height):
-        start_row(i, between)
+    for part in range(halves):
+        start_rows(part, range(1, pairs - 1))
+        for begin, end in zip(CUTS[:-1], CUTS[1:]):
+            if begin // SUBL == part:
+                entries = []
+                if begin == SUBL:
+                    entries.append(send_rows(ground, 1, SUBL, DEEP - 1 - SUBL, SUBL))
+                entries.append(send_rows(first, 1, begin, end - begin, begin))
+                far_rows.append(entries)
     near_rows = [
         send_rows(ref, 2, height - DEEP, DEEP, DEEP + height) for ref in (first, ground)
     ]
@@ -277,36 +322,75 @@
             reach = jnp.where(reach > 0.5, 1.0, 0.0)
     hops[...] = count
 
-    def finish_ring(i, own_row):
+    def finish_ring(i, own_row, only=None):
         at = slot(i)
         for number, ref in enumerate((first, ground)):
-            ring = ring_own[number, i] if own_row else ring_of(ref, at)
-            from_high = jnp.broadcast_to(ring_high[number, at], (SUBL, TILE))
-            from_low = jnp.broadcast_to(ring_low[number, at], (SUBL, TILE))
-            ring = jnp.where(at_high, from_high, jnp.where(at_low, from_low, ring))
-            ref[at, :, chunk:lanes] = ring
+            if only is not None and ref is not only:
+                continue
+            for p in (0, 1):
+                ring = ring_own[2 * number + p, i] if own_row else ring_of(ref, at, p)
+                from_high = jnp.broadcast_to(ring_high[2 * number + p, at], (SUBL, TILE))
+                from_low = jnp.broadcast_to(ring_low[2 * number + p, at], (SUBL, TILE))
+                ring = jnp.where(at_high, from_high, jnp.where(at_low, from_low, ring))
+                put_tile(ref, at, tiles + p, ring)
 
     def state(k):
         return first if k == 0 else ping if k % 2 else pong
 
+    all_tiles = range(tiles + 2)
+    lowest_lane = lane_id == 0
+    highest_lane = lane_id == TILE - 1
+
+    def row_tiles(ref, at):
+        return [tile_of(ref, at, v) for v in all_tiles]
+
+    def lower(*rows):
+        return [functools.reduce(jnp.minimum, tiles_at) for tiles_at in zip(*rows)]
+
     def least_of(low):
-        return jnp.minimum(
-            low, jnp.minimum(pltpu.roll(low, 1, 1), pltpu.roll(low, lanes - 1, 1))
-        )
+        even, odd = low[0::2], low[1::2]
+        count = len(even)
+        up = [pltpu.roll(each, 1, 1) for each in odd]
+        down = [pltpu.roll(each, TILE - 1, 1) for each in even]
+        least = []
+        for g in range(count):
+            both_of = jnp.minimum(even[g], odd[g])
+            before = up[g] if count == 1 else jnp.where(lowest_lane, up[g - 1], up[g])
+            after = down[g] if count == 1 else jnp.where(highest_lane, down[(g + 1) % count], down[g])
+            least += [jnp.minimum(both_of, before), jnp.minimum(both_of, after)]
+        return least
 
     def relax(k, begin, end):
         src, dst = state(k - 1), state(k)
         for at in range(begin, end, 2):
             count = min(2, end - at)
-            rows = [src[slot(at - 1 + j)] for j in range(count + 2)]
+            rows = [row_tiles(src, slot(at - 1 + j)) for j in range(count + 2)]
             for j in range(count):
                 above, here, below = rows[j : j + 3]
-                least = least_of(jnp.minimum(jnp.minimum(above, below), here))
-                value = jnp.maximum(ground[slot(at + j)], jnp.minimum(here, least + rise_step))
-                dst[slot(at + j)] = value
+                if count == 2:
+                    middle = lower(rows[1], rows[2]) if j == 0 else middle
+                    least = least_of(lower(middle, above if j == 0 else below))
+                else:
+                    least = least_of(lower(above, below, here))
+                values = []
+                for v in range(tiles if k == DEEP else tiles + 2):
+                    rock = tile_of(ground, slot(at + j), v)
+                    values.append(jnp.maximum(rock, jnp.minimum(here[v], least[v] + rise_step)))
+                if k == DEEP:
+                    finish_row(at + j, values)
+                    continue
+                for v, value in enumerate(values):
+                    put_tile(dst, slot(at + j), v, value)
                 if k == PASSES and 0 <= at + j < height:
-                    column_floor[0] = jnp.minimum(column_floor[0], value[:, 0:TILE])
-                    column_floor[1] = jnp.minimum(column_floor[1], value[:, chunk - TILE : chunk])
+                    column_floor[0] = jnp.minimum(column_floor[0], values[0])
+                    column_floor[1] = jnp.minimum(column_floor[1], values[tiles - 1])
+
+    def finish_row(i, values):
+        if i >= FINAL:
+            moved = shuffled([(values[2 * g], values[2 * g + 1]) for g in range(pairs)], join)
+            values = [each for pair in moved for each in pair]
+        for v, value in enumerate(values):
+            put_tile(state(DEEP), slot(i), v, value)
 
     for entry in own_ring:
         arrive(entry)
@@ -330,21 +414,32 @@
         for entry in far_rows[number]:
             arrive(entry)
         for i in range(-CUTS[number + 1], -CUTS[number]):
-            finish_ring(i, False)
-
-    for entry in far_ring + far_rows[0]:
+            finish_ring(i, False, first)
+            if -DEEP < i < -SUBL:
+                finish_ring(i, False, ground)
+
+    for entry in far_ring + [far_ground]:
         arrive(entry)
-    for i in range(SUBL):
-        at = jnp.where(sub == 0, SUBL - 1 - i, i)
-        for v in range(tiles):
-            ground[slot(-1 - i), :, v * TILE : (v + 1) * TILE] = far_elev[
-                pl.ds(at + v * SUBL, SUBL, stride=tiles * SUBL), :
-            ]
+
+    def far_start(flip):
+        for g in range(pairs):
+            rock = [turned([far_elev[natural(0, s, 2 * g + p), :] for s in range(SUBL)]) for p in (0, 1)]
+            moved = shuffled(list(zip(*rock)), split)
+            for r, pair in enumerate(moved):
+                for p in (0, 1):
+                    put_tile(ground, slot(-1 - (r if flip else SUBL - 1 - r)), 2 * g + p, pair[p])
+
+    by_side(far_start)
+    for i in range(-SUBL, 0):
+        finish_ring(i, False, ground)
+
+    for entry in far_rows[0]:
+        arrive(entry)
     for i in range(-CUTS[1], 0):
-        finish_ring(i, False)
-    strip(0, range(1, PASSES + 1))
-    for k in range(1, DEEP + 1):
-        relax(k, k if k > PASSES else height + PASSES - k, height + DEEP - k)
+        finish_ring(i, False, first)
+    for k in range(1, PASSES + 1):
+        strip(0, (k,))
+        relax(k, height + PASSES - k, height + DEEP - k)
     for number in (1, 2):
         open_strip(number)
         strip(number, range(1, PASSES + 1))
@@ -354,7 +449,7 @@
         jnp.where(last_cell, column_floor[1], unreached),
     )
     for v in range(tiles):
-        floor = jnp.minimum(floor, state(PASSES)[slot(0), :, v * TILE : (v + 1) * TILE])
+        floor = jnp.minimum(floor, tile_of(state(PASSES), slot(0), v))
     floor = jnp.min(floor, axis=(0, 1), keepdims=True)
     tile_id = tile_row * n_cols + col
     mine[...] = jnp.where(
@@ -380,33 +475,36 @@
     lax.fori_loop(1, members, spread, 0)
 
     for k in range(PASSES + 1, DEEP + 1):
-        relax(k, k - PASSES, k)
+        relax(k, k - PASSES, height + DEEP - k)
 
     def walk_at(n, r):
         return n * (n - 1) // 2 + r
 
-    entry_row = ground[slot(-1)]
-    entry_ring = jnp.where(jnp.logical_or(at_high, at_low), unreached, entry_row[:, chunk:lanes])
-    before = [jnp.concatenate([entry_row[:, 0:chunk], entry_ring], axis=1)]
+    outside_ring_cells = jnp.logical_or(at_high, at_low)
+    entry_row = row_tiles(ground, slot(-1))
+    for v in (tiles, tiles + 1):
+        entry_row[v] = jnp.where(outside_ring_cells, unreached, entry_row[v])
+    before = [entry_row]
     for n in range(1, FINAL + 1):
+        after = []
         for r in range(n):
-            low = None
-            for q in range(max(r - 1, 0), min(r + 2, len(before))):
-                row = before[q]
-                low = row if low is None else jnp.minimum(low, row)
-            walks[walk_at(n, r)] = jnp.maximum(ground[slot(r)], least_of(low) + rise_step)
-        before = [walks[walk_at(n, r)] for r in range(n)]
-
-    def seam_of(ref, at):
-        ring = ref[at, :, chunk:lanes]
-        at_first = jnp.where(right_half, ref[at, :, 0:TILE], ring)
-        at_last = jnp.where(right_half, ring, ref[at, :, chunk - TILE : chunk])
+            least = least_of(lower(*before[max(r - 1, 0) : r + 2]))
+            rock = row_tiles(ground, slot(r))
+            after.append([jnp.maximum(rock[v], least[v] + rise_step) for v in all_tiles])
+            for v in range(tiles):
+                put_tile(walks, walk_at(n, r), v, after[r][v])
+        before = after
+
+    def seam_of(ref, at, p):
+        ring = tile_of(ref, at, tiles + p)
+        at_first = jnp.where(right_half, tile_of(ref, at, p), ring)
+        at_last = jnp.where(right_half, ring, tile_of(ref, at, tiles - 2 + p))
         return jnp.where(sub_id == 0, at_first, at_last)
 
     seam_rows = list(range(-FINAL, height + FINAL))
-    for j, i in enumerate(seam_rows):
-        seam_ground[j] = seam_of(ground, slot(i))
-
+    moved = shuffled([(seam_of(ground, slot(i), 0), seam_of(ground, slot(i), 1)) for i in seam_rows], join)
+    for j, pair in enumerate(moved):
+        seam_ground[j] = jnp.where(right_half, pair[0], pair[1])
     for number in (3, 4):
         open_strip(number)
         strip(number, range(1, DEEP + 1))
@@ -448,24 +546,46 @@
             later[j] = jnp.maximum(seam_ground[j], jnp.minimum(seam[j], least + rise_step))
         seam = later
 
-    left_seam = jnp.logical_and(sub_id == 0, lane_id < FINAL)
-    right_seam = jnp.logical_and(sub_id == SUBL - 1, lane_id >= TILE - FINAL)
+    for i in range(height):
+        row = pl.ds(row_of(i), 1)
+        seam_sides[0, row, :] = seam[i + FINAL][0:1]
+        seam_sides[1, row, :] = seam[i + FINAL][SUBL - 1 : SUBL]
     tops = []
     for n in range(1, FINAL + 1):
         far_top = far_top + rise_step
         tops.append(far_top)
-    for i in range(height):
+    blocks = []
+    for i in range(FINAL):
+        values = row_tiles(state(DEEP), slot(i))
         for v in range(tiles):
-            cut = slice(v * TILE, (v + 1) * TILE)
-            top = jnp.maximum(ground[slot(i), :, cut], own_top)
             for n in range(i + 1, FINAL + 1):
-                top = jnp.minimum(top, jnp.maximum(walks[walk_at(n, i), :, cut], tops[n - 1]))
-            value = jnp.minimum(state(DEEP)[slot(i), :, cut], top)
-            if v == 0:
-                value = jnp.where(left_seam, jnp.minimum(value, seam[i + FINAL]), value)
-            if v == tiles - 1:
-                value = jnp.where(right_seam, jnp.minimum(value, seam[i + FINAL]), value)
-            out[piece(i, v)] = value
+                walk = tile_of(walks, walk_at(n, i), v)
+                values[v] = jnp.minimum(values[v], jnp.maximum(walk, tops[n - 1]))
+        blocks += [(values[2 * g], values[2 * g + 1]) for g in range(pairs)]
+    moved = shuffled(blocks, join)
+    for i in range(FINAL):
+        for v in range(tiles):
+            put_tile(state(DEEP), slot(i), v, moved[i * pairs + v // 2][v % 2])
+
+    def finish(flip):
+        for half in (range(halves - 1, -1, -1) if not flip else range(halves)):
+            for v in range(tiles):
+                order = [half * SUBL + r for r in range(SUBL)]
+                order = [height - 1 - row if flip else row for row in order]
+                rows = turned([tile_of(state(DEEP), slot(i), v) for i in order])
+                for s in range(SUBL):
+                    at = natural(half, s, v)
+                    value = jnp.minimum(rows[s], jnp.maximum(elev[at, :], own_top))
+                    at_half = slice(half * SUBL, (half + 1) * SUBL)
+                    if s == 0 and v == 0:
+                        left = jnp.minimum(value, seam_sides[0, at_half, :])
+                        value = jnp.where(lane_id < FINAL, left, value)
+                    if s == SUBL - 1 and v == tiles - 1:
+                        right = jnp.minimum(value, seam_sides[1, at_half, :])
+                        value = jnp.where(lane_id >= TILE - FINAL, right, value)
+                    out[at, :] = value
+
+    by_side(finish)
 
     for copy, side_of, dc in copies:
         when(both(side_of, dc), copy.wait_send)
@@ -486,9 +606,10 @@
         blocks = array.reshape(height // SUBL, SUBL, tiles, TILE)
         return blocks.transpose(0, 2, 1, 3).reshape(flat)
 
-    wide = pltpu.VMEM((total, SUBL, chunk + TILE), jnp.float32)
+    wide = pltpu.VMEM((total, SUBL, chunk + 2 * TILE), jnp.float32)
+    shuffle = pltpu.VMEM((2 * TILE, 2 * TILE), jnp.bfloat16)
     whole = pltpu.VMEM(flat, jnp.float32)
-    ring = pltpu.VMEM((2, total, 1, TILE), jnp.float32)
+    ring = pltpu.VMEM((4, total, 1, TILE), jnp.float32)
     marks = edge_rows.reshape(2, tiles, TILE).transpose(1, 0, 2).reshape(2 * tiles, TILE)
     operands = (tiled(elevation), tiled(fill_depth), marks, edge_sides, adjacency)
     filled = pl.pallas_call(
@@ -500,11 +621,11 @@
             whole, whole,
             pltpu.VMEM((SUBL * tiles, TILE), jnp.float32),
             wide, wide, wide, wide,
-            pltpu.VMEM((FINAL * (FINAL + 1) // 2, SUBL, chunk + TILE), jnp.float32),
+            pltpu.VMEM((FINAL * (FINAL + 1) // 2, SUBL, chunk), jnp.float32),
             pltpu.VMEM((2 * tiles, TILE), jnp.int32),
             pltpu.SMEM(edge_sides.shape, jnp.int32),
             pltpu.VMEM(adjacency.shape, jnp.int32),
-            pltpu.VMEM((2, height, SUBL, TILE), jnp.float32),
+            pltpu.VMEM((4, height, SUBL, TILE), jnp.float32),
             ring, ring,
             pltpu.VMEM((2, SUBL, TILE), jnp.float32),
             pltpu.VMEM((1, padded), jnp.float32),
@@ -512,6 +633,8 @@
             pltpu.VMEM((n_tiles, padded), jnp.float32),
             pltpu.VMEM((n_tiles, TILE), jnp.float32),
             pltpu.VMEM((height + 2 * FINAL, SUBL, TILE), jnp.float32),
+            pltpu.VMEM((2, height, TILE), jnp.float32),
+            shuffle, shuffle,
             pltpu.SemaphoreType.DMA((2 * (height // SUBL) + 3,)),
             pltpu.SemaphoreType.DMA((15,)),
             pltpu.SemaphoreType.DMA((15,)),

time: 22.2 us -> 20.7 us (0.932)
  Pallas kernels: 21.3 us -> 19.7 us
    pallas_call x1, Pallas kernels: 21.3 us -> 19.7 us  [per_device(): pl.pallas_call(functools.partial(kernel, sizes), out_shape=pltpu.VMEM(fla...]
where the time goes in v3:
time: 20.7 us; the launch traced here: 20.5 us
  Pallas kernels  19.7 us (95%)
  local copies, waits for them, and re-layouts  0.8 us (4%)
    pallas_call x1, Pallas kernels, per_device(): pl.pallas_call(functools.partial(kernel, sizes), out_shape=pltpu.VMEM(fla...  19.7 us
    unnamed x1, local copies, waits for them, and re-layouts  0.8 us

profile of v3, /device:TPU:1, one launch (start us, length us, event | category | flops | bytes accessed | tf_op | source)
XLA Modules:
  0.0 20.5 jit_solution(11221444756687279144)
XLA Ops:
  0.0 19.7 %shard_map.55 = f32[1024,128]{1,0:T(8,128)S(1)} custom-call(f32[1024,128]{1,0:T(8,128)} %bitcast.21, f32[1024,128]{1,0:T(8,128)} %bitcast.22, s32[128,128]{1,0:T(8,128)} %bitcast.23, s32[2,16]{1,0:T(2,128)} %side_hbm.1, s32[8,6]{1,0:T(8,128)} %adj_hbm.1), custom_call_target="tpu_custom_call" | custom-call | tf_op jit(solution)/shard_map/pallas_call | solution.py:615
  19.7 0.8 %copy.8 = f32[16,8192]{1,0:T(8,128)} copy(f32[16,8192]{1,0:T(8,128)S(1)} %bitcast.20) | data formatting | bytes 1048576

commit v4 on v3

--- a/solution.py
+++ b/solution.py
@@ -17,7 +17,8 @@
 spill_lift = 3.0
 
 DEEP = PASSES + FINAL
-CUTS = (0, 4, 6, 8, 10, 12)
+REACH = DEEP // 2
+CUTS = (0, 4, REACH + 1, PASSES, PASSES + 2, DEEP)
 SUBL = 8
 TILE = 128
 HALF = TILE // 2
@@ -26,7 +27,7 @@
 
 def kernel(
     sizes, elev_hbm, fill_hbm, edge_hbm, side_hbm, adj_hbm, out,
-    elev, fill, far_elev, ground, first, ping, pong, walks,
+    elev, fill, far_elev, ground, first, ping, pong, walks, times_out, times_in,
     edge, side, adj, ring_own, ring_low, ring_high, column_floor,
     mine, gathered, hops, levels, seam_ground, seam_sides, split, join,
     load_sem, send_sem, recv_sem, level_send, level_recv,
@@ -36,8 +37,9 @@
     chunk = tiles * TILE
     pairs = tiles // 2
     lanes = chunk + 2 * TILE
-    half_rows = SUBL * tiles * SUBL
-    halves = elev_hbm.shape[0] // half_rows
+    half_tiles = tiles * SUBL
+    half_rows = SUBL * half_tiles
+    halves = elev_hbm.shape[0] // half_tiles
     height = halves * SUBL
     n_tiles = adj.shape[0]
     padded = mine.shape[1]
@@ -101,7 +103,7 @@
     loads = []
     for part in range(halves):
         half = row_of(part * SUBL) // SUBL
-        at = pl.ds(pl.multiple_of(half * half_rows, half_rows), half_rows)
+        at = pl.ds(half * half_tiles, half_tiles)
         pair = []
         for number, (src, dst) in enumerate(((elev_hbm, elev), (fill_hbm, fill))):
             copy = pltpu.make_async_copy(src.at[at], dst.at[at], load_sem.at[2 * part + number])
@@ -119,7 +121,8 @@
     def outside_rows():
         for ref in (ground, first):
             ref[0:DEEP] = jnp.full((DEEP, SUBL, lanes), unreached, jnp.float32)
-        far_elev[...] = jnp.full(far_elev.shape, unreached, jnp.float32)
+        for ref in (far_elev, times_in):
+            ref[...] = jnp.full(ref.shape, unreached, jnp.float32)
 
     pl.when(jnp.logical_not(has(far)))(outside_rows)
 
@@ -187,9 +190,8 @@
                     rows[at + step] = jnp.where(stays, pltpu.roll(one, SUBL - step, 0), two)
         return rows
 
-    def natural(half, s, v):
-        at = half * half_rows + (s * tiles + v) * SUBL
-        return slice(at, at + SUBL)
+    def number_of(half, s, v):
+        return half * half_tiles + s * tiles + v
 
     def by_side(action):
         pl.when(sub == 0)(lambda: action(False))
@@ -201,8 +203,8 @@
             for g in groups:
                 here, water = {}, {}
                 for v in (2 * g, 2 * g + 1):
-                    rock = [elev[natural(half, s, v), :] for s in range(SUBL)]
-                    deep = [rock[s] + fill[natural(half, s, v), :] for s in range(SUBL)]
+                    rock = [elev[number_of(half, s, v)] for s in range(SUBL)]
+                    deep = [rock[s] + fill[number_of(half, s, v)] for s in range(SUBL)]
                     here[v], water[v] = turned(rock), turned(deep)
                     for r in range(SUBL):
                         row = half * SUBL + r
@@ -271,9 +273,9 @@
         return sent
 
     pl.semaphore_wait(barrier, members - 1)
-    far_half = row_of(0) // SUBL
-    at = pl.ds(pl.multiple_of(far_half * half_rows, half_rows), half_rows)
-    far_ground = send(elev_hbm.at[at], far_elev, 1, 0)
+    far_half = pl.ds((row_of(0) // SUBL) * half_tiles, half_tiles)
+    far_cut = pl.ds(jnp.where(sub == 0, 0, SUBL - REACH), REACH)
+    far_ground = send(elev_hbm.at[far_half, far_cut], far_elev.at[:, far_cut], 1, 0)
     side_load.wait()
     edge_load.wait()
     for pair in loads:
@@ -285,17 +287,13 @@
         start_ring(i)
     own_ring = send_ring(0, 0, height, DEEP)
     near_ring = send_ring(2, height - DEEP, DEEP, DEEP + height)
-    far_ring = send_ring(1, 0, DEEP, 0)
+    far_ring = send_ring(1, 0, REACH + 1, 0)
     far_rows = []
     for part in range(halves):
         start_rows(part, range(1, pairs - 1))
-        for begin, end in zip(CUTS[:-1], CUTS[1:]):
-            if begin // SUBL == part:
-                entries = []
-                if begin == SUBL:
-                    entries.append(send_rows(ground, 1, SUBL, DEEP - 1 - SUBL, SUBL))
-                entries.append(send_rows(first, 1, begin, end - begin, begin))
-                far_rows.append(entries)
+        if part == 0:
+            for begin, end in zip(CUTS[:2], CUTS[1:3]):
+                far_rows.append([send_rows(first, 1, begin, end - begin, begin)])
     near_rows = [
         send_rows(ref, 2, height - DEEP, DEEP, DEEP + height) for ref in (first, ground)
     ]
@@ -364,7 +362,12 @@
         src, dst = state(k - 1), state(k)
         for at in range(begin, end, 2):
             count = min(2, end - at)
-            rows = [row_tiles(src, slot(at - 1 + j)) for j in range(count + 2)]
+            rows = []
+            for i in range(at - 1, at + count + 1):
+                if i == -1 - REACH and k > 1:
+                    rows.append(row_tiles(times_in, k - 2))
+                else:
+                    rows.append(row_tiles(src, slot(i)))
             for j in range(count):
                 above, here, below = rows[j : j + 3]
                 if count == 2:
@@ -396,8 +399,14 @@
         arrive(entry)
     for i in range(height):
         finish_ring(i, True)
+    far_times = []
     for k in range(1, height // 2):
         relax(k, k, height - k)
+        if k < REACH:
+            for v, value in enumerate(row_tiles(state(k), slot(REACH))):
+                put_tile(times_out, k - 1, v, value)
+            far_times.append(send(times_out.at[k - 1], times_in.at[k - 1], 1, 0))
+    far_rows += [far_times[0:1], far_times[1:3], far_times[3:]]
 
     for entry in near_rows + near_ring:
         arrive(entry)
@@ -408,29 +417,30 @@
 
     def strip(number, passes):
         for k in passes:
-            relax(k, k - CUTS[number + 1], k - CUTS[number])
+            relax(k, max(k - CUTS[number + 1], -REACH), k - CUTS[number])
 
     def open_strip(number):
         for entry in far_rows[number]:
             arrive(entry)
-        for i in range(-CUTS[number + 1], -CUTS[number]):
-            finish_ring(i, False, first)
-            if -DEEP < i < -SUBL:
-                finish_ring(i, False, ground)
+        if number == 1:
+            for i in range(-CUTS[2], -CUTS[1]):
+                finish_ring(i, False, first)
 
     for entry in far_ring + [far_ground]:
         arrive(entry)
 
     def far_start(flip):
         for g in range(pairs):
-            rock = [turned([far_elev[natural(0, s, 2 * g + p), :] for s in range(SUBL)]) for p in (0, 1)]
+            rock = [turned([far_elev[number_of(0, s, 2 * g + p)] for s in range(SUBL)]) for p in (0, 1)]
             moved = shuffled(list(zip(*rock)), split)
             for r, pair in enumerate(moved):
+                i = -1 - (r if flip else SUBL - 1 - r)
                 for p in (0, 1):
-                    put_tile(ground, slot(-1 - (r if flip else SUBL - 1 - r)), 2 * g + p, pair[p])
+                    if i >= -REACH:
+                        put_tile(ground, slot(i), 2 * g + p, pair[p])
 
     by_side(far_start)
-    for i in range(-SUBL, 0):
+    for i in range(-REACH, 0):
         finish_ring(i, False, ground)
 
     for entry in far_rows[0]:
@@ -574,8 +584,8 @@
                 order = [height - 1 - row if flip else row for row in order]
                 rows = turned([tile_of(state(DEEP), slot(i), v) for i in order])
                 for s in range(SUBL):
-                    at = natural(half, s, v)
-                    value = jnp.minimum(rows[s], jnp.maximum(elev[at, :], own_top))
+                    at = number_of(half, s, v)
+                    value = jnp.minimum(rows[s], jnp.maximum(elev[at], own_top))
                     at_half = slice(half * SUBL, (half + 1) * SUBL)
                     if s == 0 and v == 0:
                         left = jnp.minimum(value, seam_sides[0, at_half, :])
@@ -583,7 +593,7 @@
                     if s == SUBL - 1 and v == tiles - 1:
                         right = jnp.minimum(value, seam_sides[1, at_half, :])
                         value = jnp.where(lane_id >= TILE - FINAL, right, value)
-                    out[at, :] = value
+                    out[at] = value
 
     by_side(finish)
 
@@ -600,7 +610,7 @@
     members = sizes[1] * sizes[2] * sizes[3]
     n_tiles = adjacency.shape[0]
     padded = -(-n_tiles // TILE) * TILE
-    flat = (height * tiles, TILE)
+    flat = (height * tiles // SUBL, SUBL, TILE)
 
     def tiled(array):
         blocks = array.reshape(height // SUBL, SUBL, tiles, TILE)
@@ -609,6 +619,7 @@
     wide = pltpu.VMEM((total, SUBL, chunk + 2 * TILE), jnp.float32)
     shuffle = pltpu.VMEM((2 * TILE, 2 * TILE), jnp.bfloat16)
     whole = pltpu.VMEM(flat, jnp.float32)
+    times = pltpu.VMEM((REACH - 1, SUBL, chunk + 2 * TILE), jnp.float32)
     ring = pltpu.VMEM((4, total, 1, TILE), jnp.float32)
     marks = edge_rows.reshape(2, tiles, TILE).transpose(1, 0, 2).reshape(2 * tiles, TILE)
     operands = (tiled(elevation), tiled(fill_depth), marks, edge_sides, adjacency)
@@ -619,9 +630,10 @@
         out_specs=pl.BlockSpec(memory_space=pltpu.VMEM),
         scratch_shapes=[
             whole, whole,
-            pltpu.VMEM((SUBL * tiles, TILE), jnp.float32),
+            pltpu.VMEM((tiles, SUBL, TILE), jnp.float32),
             wide, wide, wide, wide,
             pltpu.VMEM((FINAL * (FINAL + 1) // 2, SUBL, chunk), jnp.float32),
+            times, times,
             pltpu.VMEM((2 * tiles, TILE), jnp.int32),
             pltpu.SMEM(edge_sides.shape, jnp.int32),
             pltpu.VMEM(adjacency.shape, jnp.int32),
@@ -636,8 +648,8 @@
             pltpu.VMEM((2, height, TILE), jnp.float32),
             shuffle, shuffle,
             pltpu.SemaphoreType.DMA((2 * (height // SUBL) + 3,)),
-            pltpu.SemaphoreType.DMA((15,)),
-            pltpu.SemaphoreType.DMA((15,)),
+            pltpu.SemaphoreType.DMA((16,)),
+            pltpu.SemaphoreType.DMA((16,)),
             pltpu.SemaphoreType.DMA,
             pltpu.SemaphoreType.DMA,
         ],

time: 20.7 us -> 19.7 us (0.952)
  Pallas kernels: 19.7 us -> 18.6 us
    pallas_call x1, Pallas kernels: 19.7 us -> 18.6 us  [per_device(): pl.pallas_call(functools.partial(kernel, sizes), out_shape=pltpu.VMEM(fla...]
where the time goes in v4:
time: 19.7 us; the launch traced here: 19.4 us
  Pallas kernels  18.6 us (94%)
  local copies, waits for them, and re-layouts  0.8 us (4%)
    pallas_call x1, Pallas kernels, per_device(): pl.pallas_call(functools.partial(kernel, sizes), out_shape=pltpu.VMEM(fla...  18.6 us
    unnamed x1, local copies, waits for them, and re-layouts  0.8 us

profile of v4, /device:TPU:1, one launch (start us, length us, event | category | flops | bytes accessed | tf_op | source)
XLA Modules:
  0.0 19.4 jit_solution(7606047773596794611)
XLA Ops:
  0.0 18.6 %shard_map.55 = f32[128,8,128]{2,1,0:T(8,128)S(1)} custom-call(f32[128,8,128]{2,1,0:T(8,128)} %bitcast.21, f32[128,8,128]{2,1,0:T(8,128)} %bitcast.22, s32[128,128]{1,0:T(8,128)} %bitcast.23, s32[2,16]{1,0:T(2,128)} %side_hbm.1, s32[8,6]{1,0:T(8,128)} %adj_hbm.1), custom_call_target="tpu_custom_call" | custom-call | tf_op jit(solution)/shard_map/pallas_call | solution.py:626
  18.6 0.8 %copy.8 = f32[16,8192]{1,0:T(8,128)} copy(f32[16,8192]{1,0:T(8,128)S(1)} %bitcast.20) | data formatting | bytes 1048576

commit v5 on v4

--- a/solution.py
+++ b/solution.py
@@ -19,6 +19,7 @@
 DEEP = PASSES + FINAL
 REACH = DEEP // 2
 CUTS = (0, 4, REACH + 1, PASSES, PASSES + 2, DEEP)
+MOST_UNROLLED = 16
 SUBL = 8
 TILE = 128
 HALF = TILE // 2
@@ -99,7 +100,7 @@
         )
         return carry
 
-    lax.fori_loop(1, members, greet, 0)
+    lax.fori_loop(1, members, greet, 0, unroll=members <= MOST_UNROLLED)
     loads = []
     for part in range(halves):
         half = row_of(part * SUBL) // SUBL
@@ -450,6 +451,16 @@
     for k in range(1, PASSES + 1):
         strip(0, (k,))
         relax(k, height + PASSES - k, height + DEEP - k)
+    def seam_of(ref, at, p):
+        ring = tile_of(ref, at, tiles + p)
+        at_first = jnp.where(right_half, tile_of(ref, at, p), ring)
+        at_last = jnp.where(right_half, ring, tile_of(ref, at, tiles - 2 + p))
+        return jnp.where(sub_id == 0, at_first, at_last)
+
+    seam_rows = list(range(-FINAL, height + FINAL))
+    moved = shuffled([(seam_of(ground, slot(i), 0), seam_of(ground, slot(i), 1)) for i in seam_rows], join)
+    for j, pair in enumerate(moved):
+        seam_ground[j] = jnp.where(right_half, pair[0], pair[1])
     for number in (1, 2):
         open_strip(number)
         strip(number, range(1, PASSES + 1))
@@ -482,7 +493,7 @@
         level_copy(step).start()
         return carry
 
-    lax.fori_loop(1, members, spread, 0)
+    lax.fori_loop(1, members, spread, 0, unroll=members <= MOST_UNROLLED)
 
     for k in range(PASSES + 1, DEEP + 1):
         relax(k, k - PASSES, height + DEEP - k)
@@ -505,16 +516,6 @@
                 put_tile(walks, walk_at(n, r), v, after[r][v])
         before = after
 
-    def seam_of(ref, at, p):
-        ring = tile_of(ref, at, tiles + p)
-        at_first = jnp.where(right_half, tile_of(ref, at, p), ring)
-        at_last = jnp.where(right_half, ring, tile_of(ref, at, tiles - 2 + p))
-        return jnp.where(sub_id == 0, at_first, at_last)
-
-    seam_rows = list(range(-FINAL, height + FINAL))
-    moved = shuffled([(seam_of(ground, slot(i), 0), seam_of(ground, slot(i), 1)) for i in seam_rows], join)
-    for j, pair in enumerate(moved):
-        seam_ground[j] = jnp.where(right_half, pair[0], pair[1])
     for number in (3, 4):
         open_strip(number)
         strip(number, range(1, DEEP + 1))

time: 19.7 us -> 19.4 us (0.985)
  Pallas kernels: 18.6 us -> 18.3 us
    pallas_call x1, Pallas kernels: 18.6 us -> 18.3 us  [per_device(): pl.pallas_call(functools.partial(kernel, sizes), out_shape=pltpu.VMEM(fla...]
where the time goes in v5:
time: 19.4 us; the launch traced here: 19.1 us
  Pallas kernels  18.3 us (94%)
  local copies, waits for them, and re-layouts  0.8 us (4%)
    pallas_call x1, Pallas kernels, per_device(): pl.pallas_call(functools.partial(kernel, sizes), out_shape=pltpu.VMEM(fla...  18.3 us
    unnamed x1, local copies, waits for them, and re-layouts  0.8 us

profile of v5, /device:TPU:1, one launch (start us, length us, event | category | flops | bytes accessed | tf_op | source)
XLA Modules:
  0.0 19.1 jit_solution(16797821212983807927)
XLA Ops:
  0.0 18.3 %shard_map.55 = f32[128,8,128]{2,1,0:T(8,128)S(1)} custom-call(f32[128,8,128]{2,1,0:T(8,128)} %bitcast.21, f32[128,8,128]{2,1,0:T(8,128)} %bitcast.22, s32[128,128]{1,0:T(8,128)} %bitcast.23, s32[2,16]{1,0:T(2,128)} %side_hbm.1, s32[8,6]{1,0:T(8,128)} %adj_hbm.1), custom_call_target="tpu_custom_call" | custom-call | tf_op jit(solution)/shard_map/pallas_call | solution.py:627
  18.3 0.8 %copy.8 = f32[16,8192]{1,0:T(8,128)} copy(f32[16,8192]{1,0:T(8,128)S(1)} %bitcast.20) | data formatting | bytes 1048576
